TPU v7x, 32 devices: a whole 2x2x4 slice. The times are simulated.
32 devices in a mesh: parts: 2 (over x), seq: 16 (over z, y, core).
Axes of the slice: x: 2, y: 2, z: 4, core: 2. Of those that a mesh axis runs over, the one named last changes fastest.
Arguments:
- queries: bfloat16 [2, 4, 8192], P(None, 'parts'), parts along dimension 1, may hold values from -7 to 7
- cache_k: bfloat16 [65536, 1024], P(('parts', 'seq')), parts along dimension 0, may hold values from -15 to 15
- cache_v: bfloat16 [65536, 1024], P(('parts', 'seq')), parts along dimension 0, may hold values from -6 to 6
- context_len: int32 [4], P('parts'), parts along dimension 0, may hold values from 8192 to 16384, as said below
- slot_seq: int32 [65536], P(('parts', 'seq')), parts along dimension 0, may hold values from 0 to 2, as said below
- slot_pos: int32 [65536], P(('parts', 'seq')), parts along dimension 0, may hold values from 0 to 16383, as said below
Outputs:
- attended: bfloat16 [2, 4, 8192], P(None, 'parts'), parts along dimension 1
There are 2 independent parts, one for each index of `parts`. A program takes and returns all parts, laid end to end along the dimension named above; each array names one. Nothing has to cross between parts.
Inputs may be any that keep to these rules, and one draw needn't show every extreme that they name: Each sequence s has exactly context_len[s] slots with slot_seq = s; some sequence has exactly 16384. `slot_seq`: aligned blocks of 128 slots belong to one sequence or are free; the slots of a sequence hold each position from 0 to context_len[s] - 1 exactly once; free slots carry 2. `slot_pos`: 0 on free slots.
All inputs are finite; a program needn't handle non-finite values.
Results may differ from a plain program's by a relative error of at most 0.006.
Values may be sent and summed in bfloat16 or wider, within the bound.
A program may use at most 64 MiB of HBM per device.

v0:
```python
import jax
import jax.numpy as jnp
from jax import lax
from jax.sharding import PartitionSpec as P

QH = 64
KVH = 8
HD = 128
GROUP = 8


def merged(array, axis, combine):
    everything = jax.tree.map(lambda part: lax.all_gather(part, axis), array)
    first = jax.tree.map(lambda part: part[0], everything)

    def step(k, so_far):
        return combine(so_far, jax.tree.map(lambda part: part[k], everything))

    return lax.fori_loop(1, lax.axis_size(axis), step, first)


def combine(first, second):
    max_a, denom_a, numer_a = first
    max_b, denom_b, numer_b = second
    highest = jnp.maximum(max_a, max_b)
    factor_a = jnp.exp(max_a - highest)
    factor_b = jnp.exp(max_b - highest)
    return (
        highest,
        denom_a * factor_a + denom_b * factor_b,
        numer_a * factor_a[..., None] + numer_b * factor_b[..., None],
    )


def shard_terms(scores, allowed, shift, value_rows):
    weights = jnp.where(allowed, jnp.exp(scores - shift[..., None]), jnp.float32(0.0))
    denom = jnp.sum(weights, axis=-1)
    numer = jnp.einsum(
        "tsghn,ngd->tsghd",
        weights.astype(jnp.bfloat16),
        value_rows,
        preferred_element_type=jnp.float32,
    )
    return (denom, numer)


def per_device(queries, cache_k, cache_v, context_len, slot_seq, slot_pos):
    slot_count = cache_k.shape[0]
    seq_count = queries.shape[1]
    query_heads = queries.reshape(2, seq_count, KVH, GROUP, HD)
    key_rows = cache_k.reshape(slot_count, KVH, HD)
    value_rows = cache_v.reshape(slot_count, KVH, HD)
    scores = jnp.einsum(
        "tsghd,ngd->tsghn", query_heads, key_rows, preferred_element_type=jnp.float32
    )
    scores = scores * HD ** (-0.5)
    seq_ids = jnp.arange(seq_count, dtype=jnp.int32)
    step_ids = jnp.arange(2, dtype=jnp.int32)
    owners = slot_seq[None, :] == seq_ids[:, None]
    last_visible = context_len[None, :] - 2 + step_ids[:, None]
    allowed = owners[None, :, :] & (slot_pos[None, None, :] <= last_visible[:, :, None])
    allowed = allowed[:, :, None, None, :]
    local_max = jnp.max(jnp.where(allowed, scores, jnp.float32(-1e30)), axis=-1)
    denom, numer = shard_terms(scores, allowed, local_max, value_rows)
    highest, denom, numer = merged((local_max, denom, numer), "seq", combine)
    attended = (numer / denom[..., None]).astype(jnp.bfloat16)
    return attended.reshape(2, seq_count, QH * HD)


def solution(mesh):
    return jax.shard_map(
        per_device,
        mesh=mesh,
        in_specs=(
            P(None, "parts", None),
            P(("parts", "seq"), None),
            P(("parts", "seq"), None),
            P("parts"),
            P(("parts", "seq")),
            P(("parts", "seq")),
        ),
        out_specs=P(None, "parts", None),
        check_vma=False,
    )
```

profile of v0, /device:TPU:0, one launch (start us, length us, event | category | flops | bytes accessed | tf_op | source)
XLA Modules:
  0.0 90.8 jit_solution(8576119718643582524)
XLA Ops:
  6.5 0.0 all-gather.5.cloned.1.call-start
  6.5 0.7 iota_compare_fusion
  7.2 0.7 broadcast_add_fusion
  7.9 0.0 copy-start.1
  7.9 5.3 %copy.27 = bf16[256,8,8,128]{3,2,1,0:T(8,128)(2,1)} copy(bf16[256,8,8,128]{3,1,2,0:T(8,128)(2,1)} %bitcast.39) | data formatting | bytes 8388608
  13.2 0.0 copy-done.1
  13.2 0.1 reshape.60
  13.2 0.0 copy-start.2
  13.2 0.0 copy-start
  13.3 3.5 %copy.28 = bf16[256,8,8,128]{3,2,1,0:T(8,128)(2,1)S(1)} copy(bf16[256,8,8,128]{3,1,2,0:T(8,128)(2,1)} %bitcast.40) | data formatting | bytes 8388608
  16.7 0.0 copy-done.2
  16.7 0.1 compare_and_fusion
  16.8 0.0 copy-done
  16.8 1.7 %select_reduce_fusion = (f32[2,2,8,8]{3,1,0,2:T(2,128)S(1)}, f32[2,2,8,8,2048]{4,3,1,0,2:T(8,128)S(1)}) fusion(pred[2,2,2048]{2,1,0:T(4,128)(4,1)S(1)} %compare_and_fusion, bf16[2,2,8,8,128]{4,3,2,1,0:T(8,128)(2,1)S(1)} %reshape.60, bf16[2048,8,128,1,1]{2,1,0,4,3:T(8,128)(2,1)S(1)} %bitcast.38), kind=kOutput, calls=%fused_computation.17 | convolution fusion | flops 135790336 | bytes 6366208 | tf_op jit(solution)/shard_map/tsghd,ngd->tsghn/dot_general | solution.py:53
  18.5 2.1 %fusion.16 = f32[2,2,8,8,128]{4,3,1,0,2:T(8,128)} fusion(bf16[2048,8,128,1,1]{2,1,0,4,3:T(8,128)(2,1)S(1)} %bitcast.41, f32[2,2,8,8,2048]{4,3,1,0,2:T(8,128)S(1)} %get-tuple-element.217, f32[2,2,8,8]{3,1,0,2:T(2,128)S(1)} %get-tuple-element.216, pred[2,2,2048]{2,1,0:T(4,128)(4,1)S(1)} %compare_and_fusion), kind=kOutput, calls=%fused_computation.20 | convolution fusion | flops 135790592 | bytes 6431744 | tf_op jit(solution)/shard_map/tsghn,ngd->tsghd/dot_general | solution.py:38
  20.6 0.0 all-gather.5.cloned.1.call-update
  20.7 0.6 fusion.15
  21.2 24.1 %all-gather.1 = f32[32,2,8,8]{3,2,1,0:T(8,128)S(1)} all-gather(f32[2,2,8,8]{3,2,1,0:T(8,128)S(1)} %copy.16), channel_id=3, replica_groups=mesh['parts'=2,'seq'=16] {'seq'}, dimensions={0}, use_global_device_ids=true | all-gather | bytes 17408 | tf_op jit(solution)/shard_map/all_gather | solution.py:13
  45.4 18.6 %all-gather = f32[32,2,8,8]{3,2,1,0:T(8,128)S(1)} all-gather(f32[2,2,8,8]{3,2,1,0:T(8,128)S(1)} %copy.15), channel_id=2, replica_groups=mesh['parts'=2,'seq'=16] {'seq'}, dimensions={0}, use_global_device_ids=true | all-gather | bytes 17408 | tf_op jit(solution)/shard_map/all_gather | solution.py:13
  64.0 1.3 %all-gather.5.cloned.1.call-done = f32[32,2,8,8,128]{4,3,1,0,2:T(8,128)} async-done(((f32[2,2,8,8,128]{4,3,1,0,2:T(8,128)}), f32[32,2,8,8,128]{4,3,1,0,2:T(8,128)}) %all-gather.5.cloned.1.call-update) | async-done | bytes 2097168 | tf_op jit(solution)/shard_map/all_gather | solution.py:13
  65.3 0.9 %slice.17 = f32[2,2,8,8,128]{4,3,1,0,2:T(8,128)S(1)} slice(f32[32,2,8,8,128]{4,3,1,0,2:T(8,128)} %all-gather.5.cloned.1.call-done), slice={[0:2], [0:2], [0:8], [0:8], [0:128]} | slice | bytes 262144 | tf_op jit(solution)/shard_map/slice | solution.py:14
  66.2 17.0 %while.19 = (s32[]{:T(128)}, f32[2,2,8,8]{3,2,1,0:T(8,128)S(1)}, f32[2,2,8,8]{3,2,1,0:T(8,128)S(1)}, f32[2,2,8,8,128]{4,3,2,1,0:T(8,128)S(1)}, f32[16,2,2,8,8]{4...) while((s32[]{:T(128)}, f32[2,2,8,8]{3,2,1,0:T(8,128)S(1)}, ...), condition=%wide.region_3.4_spmd, body=%wide.region_2.3_spmd.sunk | while | flops 99845 | bytes 403607 | solution.py:19
  66.3 1.1 %fusion.29 = f32[2,2,8,8,128]{4,3,2,1,0:T(8,128)S(1)} fusion(f32[2,2,8,8,128]{4,3,2,1,0:T(8,128)S(1)} %get-tuple-element.282, f32[2,2,8,8]{3,2,1,0:T(8,128)S(1)} %get-tuple-element.267, f32[2,2,8,8]{3,2,1,0:T(8,128)S(1)} %get-tuple-element.268, f32[16,2,2,8,8,128]{5,4,2,1,0,3:T(8,128)} %get-tuple-element.295, s32[]{:T(128)S(6)} %select_n.29), kind=kLoop, calls=%fused_computation.2.clone.1 | loop fusion | flops 98304 | bytes 395268 | tf_op jit(solution)/shard_map/while/body/eval_jaxpr/add | solution.py:31
  67.4 1.1 %fusion.29 = f32[2,2,8,8,128]{4,3,2,1,0:T(8,128)S(1)} fusion(f32[2,2,8,8,128]{4,3,2,1,0:T(8,128)S(1)} %get-tuple-element.282, f32[2,2,8,8]{3,2,1,0:T(8,128)S(1)} %get-tuple-element.267, f32[2,2,8,8]{3,2,1,0:T(8,128)S(1)} %get-tuple-element.268, f32[16,2,2,8,8,128]{5,4,2,1,0,3:T(8,128)} %get-tuple-element.295, s32[]{:T(128)S(6)} %select_n.29), kind=kLoop, calls=%fused_computation.2.clone.1 | loop fusion | flops 98304 | bytes 395268 | tf_op jit(solution)/shard_map/while/body/eval_jaxpr/add | solution.py:31
  68.5 1.1 %fusion.29 = f32[2,2,8,8,128]{4,3,2,1,0:T(8,128)S(1)} fusion(f32[2,2,8,8,128]{4,3,2,1,0:T(8,128)S(1)} %get-tuple-element.282, f32[2,2,8,8]{3,2,1,0:T(8,128)S(1)} %get-tuple-element.267, f32[2,2,8,8]{3,2,1,0:T(8,128)S(1)} %get-tuple-element.268, f32[16,2,2,8,8,128]{5,4,2,1,0,3:T(8,128)} %get-tuple-element.295, s32[]{:T(128)S(6)} %select_n.29), kind=kLoop, calls=%fused_computation.2.clone.1 | loop fusion | flops 98304 | bytes 395268 | tf_op jit(solution)/shard_map/while/body/eval_jaxpr/add | solution.py:31
  69.6 1.1 %fusion.29 = f32[2,2,8,8,128]{4,3,2,1,0:T(8,128)S(1)} fusion(f32[2,2,8,8,128]{4,3,2,1,0:T(8,128)S(1)} %get-tuple-element.282, f32[2,2,8,8]{3,2,1,0:T(8,128)S(1)} %get-tuple-element.267, f32[2,2,8,8]{3,2,1,0:T(8,128)S(1)} %get-tuple-element.268, f32[16,2,2,8,8,128]{5,4,2,1,0,3:T(8,128)} %get-tuple-element.295, s32[]{:T(128)S(6)} %select_n.29), kind=kLoop, calls=%fused_computation.2.clone.1 | loop fusion | flops 98304 | bytes 395268 | tf_op jit(solution)/shard_map/while/body/eval_jaxpr/add | solution.py:31
  70.8 1.1 %fusion.29 = f32[2,2,8,8,128]{4,3,2,1,0:T(8,128)S(1)} fusion(f32[2,2,8,8,128]{4,3,2,1,0:T(8,128)S(1)} %get-tuple-element.282, f32[2,2,8,8]{3,2,1,0:T(8,128)S(1)} %get-tuple-element.267, f32[2,2,8,8]{3,2,1,0:T(8,128)S(1)} %get-tuple-element.268, f32[16,2,2,8,8,128]{5,4,2,1,0,3:T(8,128)} %get-tuple-element.295, s32[]{:T(128)S(6)} %select_n.29), kind=kLoop, calls=%fused_computation.2.clone.1 | loop fusion | flops 98304 | bytes 395268 | tf_op jit(solution)/shard_map/while/body/eval_jaxpr/add | solution.py:31
  71.9 1.1 %fusion.29 = f32[2,2,8,8,128]{4,3,2,1,0:T(8,128)S(1)} fusion(f32[2,2,8,8,128]{4,3,2,1,0:T(8,128)S(1)} %get-tuple-element.282, f32[2,2,8,8]{3,2,1,0:T(8,128)S(1)} %get-tuple-element.267, f32[2,2,8,8]{3,2,1,0:T(8,128)S(1)} %get-tuple-element.268, f32[16,2,2,8,8,128]{5,4,2,1,0,3:T(8,128)} %get-tuple-element.295, s32[]{:T(128)S(6)} %select_n.29), kind=kLoop, calls=%fused_computation.2.clone.1 | loop fusion | flops 98304 | bytes 395268 | tf_op jit(solution)/shard_map/while/body/eval_jaxpr/add | solution.py:31
  73.0 1.1 %fusion.29 = f32[2,2,8,8,128]{4,3,2,1,0:T(8,128)S(1)} fusion(f32[2,2,8,8,128]{4,3,2,1,0:T(8,128)S(1)} %get-tuple-element.282, f32[2,2,8,8]{3,2,1,0:T(8,128)S(1)} %get-tuple-element.267, f32[2,2,8,8]{3,2,1,0:T(8,128)S(1)} %get-tuple-element.268, f32[16,2,2,8,8,128]{5,4,2,1,0,3:T(8,128)} %get-tuple-element.295, s32[]{:T(128)S(6)} %select_n.29), kind=kLoop, calls=%fused_computation.2.clone.1 | loop fusion | flops 98304 | bytes 395268 | tf_op jit(solution)/shard_map/while/body/eval_jaxpr/add | solution.py:31
  74.2 1.1 %fusion.29 = f32[2,2,8,8,128]{4,3,2,1,0:T(8,128)S(1)} fusion(f32[2,2,8,8,128]{4,3,2,1,0:T(8,128)S(1)} %get-tuple-element.282, f32[2,2,8,8]{3,2,1,0:T(8,128)S(1)} %get-tuple-element.267, f32[2,2,8,8]{3,2,1,0:T(8,128)S(1)} %get-tuple-element.268, f32[16,2,2,8,8,128]{5,4,2,1,0,3:T(8,128)} %get-tuple-element.295, s32[]{:T(128)S(6)} %select_n.29), kind=kLoop, calls=%fused_computation.2.clone.1 | loop fusion | flops 98304 | bytes 395268 | tf_op jit(solution)/shard_map/while/body/eval_jaxpr/add | solution.py:31
  75.3 1.1 %fusion.29 = f32[2,2,8,8,128]{4,3,2,1,0:T(8,128)S(1)} fusion(f32[2,2,8,8,128]{4,3,2,1,0:T(8,128)S(1)} %get-tuple-element.282, f32[2,2,8,8]{3,2,1,0:T(8,128)S(1)} %get-tuple-element.267, f32[2,2,8,8]{3,2,1,0:T(8,128)S(1)} %get-tuple-element.268, f32[16,2,2,8,8,128]{5,4,2,1,0,3:T(8,128)} %get-tuple-element.295, s32[]{:T(128)S(6)} %select_n.29), kind=kLoop, calls=%fused_computation.2.clone.1 | loop fusion | flops 98304 | bytes 395268 | tf_op jit(solution)/shard_map/while/body/eval_jaxpr/add | solution.py:31
  76.4 1.1 %fusion.29 = f32[2,2,8,8,128]{4,3,2,1,0:T(8,128)S(1)} fusion(f32[2,2,8,8,128]{4,3,2,1,0:T(8,128)S(1)} %get-tuple-element.282, f32[2,2,8,8]{3,2,1,0:T(8,128)S(1)} %get-tuple-element.267, f32[2,2,8,8]{3,2,1,0:T(8,128)S(1)} %get-tuple-element.268, f32[16,2,2,8,8,128]{5,4,2,1,0,3:T(8,128)} %get-tuple-element.295, s32[]{:T(128)S(6)} %select_n.29), kind=kLoop, calls=%fused_computation.2.clone.1 | loop fusion | flops 98304 | bytes 395268 | tf_op jit(solution)/shard_map/while/body/eval_jaxpr/add | solution.py:31
  77.6 1.1 %fusion.29 = f32[2,2,8,8,128]{4,3,2,1,0:T(8,128)S(1)} fusion(f32[2,2,8,8,128]{4,3,2,1,0:T(8,128)S(1)} %get-tuple-element.282, f32[2,2,8,8]{3,2,1,0:T(8,128)S(1)} %get-tuple-element.267, f32[2,2,8,8]{3,2,1,0:T(8,128)S(1)} %get-tuple-element.268, f32[16,2,2,8,8,128]{5,4,2,1,0,3:T(8,128)} %get-tuple-element.295, s32[]{:T(128)S(6)} %select_n.29), kind=kLoop, calls=%fused_computation.2.clone.1 | loop fusion | flops 98304 | bytes 395268 | tf_op jit(solution)/shard_map/while/body/eval_jaxpr/add | solution.py:31
  78.7 1.1 %fusion.29 = f32[2,2,8,8,128]{4,3,2,1,0:T(8,128)S(1)} fusion(f32[2,2,8,8,128]{4,3,2,1,0:T(8,128)S(1)} %get-tuple-element.282, f32[2,2,8,8]{3,2,1,0:T(8,128)S(1)} %get-tuple-element.267, f32[2,2,8,8]{3,2,1,0:T(8,128)S(1)} %get-tuple-element.268, f32[16,2,2,8,8,128]{5,4,2,1,0,3:T(8,128)} %get-tuple-element.295, s32[]{:T(128)S(6)} %select_n.29), kind=kLoop, calls=%fused_computation.2.clone.1 | loop fusion | flops 98304 | bytes 395268 | tf_op jit(solution)/shard_map/while/body/eval_jaxpr/add | solution.py:31
  79.8 1.1 %fusion.29 = f32[2,2,8,8,128]{4,3,2,1,0:T(8,128)S(1)} fusion(f32[2,2,8,8,128]{4,3,2,1,0:T(8,128)S(1)} %get-tuple-element.282, f32[2,2,8,8]{3,2,1,0:T(8,128)S(1)} %get-tuple-element.267, f32[2,2,8,8]{3,2,1,0:T(8,128)S(1)} %get-tuple-element.268, f32[16,2,2,8,8,128]{5,4,2,1,0,3:T(8,128)} %get-tuple-element.295, s32[]{:T(128)S(6)} %select_n.29), kind=kLoop, calls=%fused_computation.2.clone.1 | loop fusion | flops 98304 | bytes 395268 | tf_op jit(solution)/shard_map/while/body/eval_jaxpr/add | solution.py:31
  81.0 1.1 %fusion.29 = f32[2,2,8,8,128]{4,3,2,1,0:T(8,128)S(1)} fusion(f32[2,2,8,8,128]{4,3,2,1,0:T(8,128)S(1)} %get-tuple-element.282, f32[2,2,8,8]{3,2,1,0:T(8,128)S(1)} %get-tuple-element.267, f32[2,2,8,8]{3,2,1,0:T(8,128)S(1)} %get-tuple-element.268, f32[16,2,2,8,8,128]{5,4,2,1,0,3:T(8,128)} %get-tuple-element.295, s32[]{:T(128)S(6)} %select_n.29), kind=kLoop, calls=%fused_computation.2.clone.1 | loop fusion | flops 98304 | bytes 395268 | tf_op jit(solution)/shard_map/while/body/eval_jaxpr/add | solution.py:31
  82.1 1.1 %fusion.29 = f32[2,2,8,8,128]{4,3,2,1,0:T(8,128)S(1)} fusion(f32[2,2,8,8,128]{4,3,2,1,0:T(8,128)S(1)} %get-tuple-element.282, f32[2,2,8,8]{3,2,1,0:T(8,128)S(1)} %get-tuple-element.267, f32[2,2,8,8]{3,2,1,0:T(8,128)S(1)} %get-tuple-element.268, f32[16,2,2,8,8,128]{5,4,2,1,0,3:T(8,128)} %get-tuple-element.295, s32[]{:T(128)S(6)} %select_n.29), kind=kLoop, calls=%fused_computation.2.clone.1 | loop fusion | flops 98304 | bytes 395268 | tf_op jit(solution)/shard_map/while/body/eval_jaxpr/add | solution.py:31
  83.2 0.1 divide_convert_fusion
  83.3 0.6 reshape.62
  (21 shorter events, 0.4 us)
Async XLA Ops:
  6.5 58.7 %all-gather.5.cloned.1.call-start = ((), (), s32[]{:S(2)}) async-start(), calls=%async_computation | async-start | bytes 2228224 | tf_op jit(solution)/shard_map/all_gather | solution.py:13
  7.9 5.3 %copy-start.1 = (bf16[2,2,8192]{2,1,0:T(2,128)(2,1)S(1)}, bf16[2,2,8192]{2,1,0:T(2,128)(2,1)}, u32[]{:S(2)}) copy-start(bf16[2,2,8192]{2,1,0:T(2,128)(2,1)} %param.8) | copy-start | bytes 196612
  13.2 3.5 %copy-start.2 = (s32[2048]{0:T(1024)S(1)}, s32[2048]{0:T(1024)}, u32[]{:S(2)}) copy-start(s32[2048]{0:T(1024)} %param.13) | copy-start | bytes 24580
  13.2 3.6 %copy-start = (bf16[256,8,8,128]{3,2,1,0:T(8,128)(2,1)S(1)}, bf16[256,8,8,128]{3,2,1,0:T(8,128)(2,1)}, u32[]{:S(2)}) copy-start(bf16[256,8,8,128]{3,2,1,0:T(8,128)(2,1)} %copy.27) | copy-start | bytes 12582916
Sparse Core Ops, SparseCore 0:
  20.8 44.4 all-gather.4
where the time goes:
time: 91.3 us; the launch traced here: 90.8 us
  blocking collectives  42.8 us (47%)
  other arithmetic  18.6 us (20%)
  between operations  13.5 us (15%)
  local copies, waits for them, and re-layouts  10.4 us (11%)
  matrix products  3.79 us (4%)
  waiting for transfers between devices  1.29 us (1%)
    all_gather x2, blocking collectives, merged(): everything = jax.tree.map(lambda part: lax.all_gather(part, axis), array)  42.8 us
    add x15, other arithmetic, combine(): numer_a * factor_a[..., None] + numer_b * factor_b[..., None]  16.2 us
    unnamed x8, local copies, waits for them, and re-layouts  8.73 us
    dot_general x1, matrix products, shard_terms(): jnp.einsum('tsghn,ngd->tsghd', weights.astype(jnp.bfloat16), value_rows,...  2.11 us
  transfers between devices with their start and end apart: 1, of which 1 were waited for; matrix products, arithmetic and copies ran while one was open for 1% of the time, Pallas kernels for 0%

commit v1 on v0

v1 whole, which is shorter than its diff:
```python
import functools

import jax
import jax.numpy as jnp
from jax import lax
from jax.experimental import pallas as pl
from jax.experimental.pallas import tpu as pltpu
from jax.sharding import PartitionSpec as P

KVH = 8
HD = 128
INNER = 4
SHIFT = HD ** (-0.5) * 1.4426950408889634
HIDDEN = -1e30
MESH = pl.DeviceIdType.MESH


def rows_to_columns(rows):
    return jnp.transpose(rows)


def scaled_sum(ml, numer_refs, count, rows, final):
    maxima = [ml(i)[0:1, :] for i in range(count)]
    denoms = [ml(i)[1:2, :] for i in range(count)]
    top = functools.reduce(jnp.maximum, maxima)
    factors = [jnp.exp2((m - top) * SHIFT) for m in maxima]
    denom = sum(f * d for f, d in zip(factors, denoms))
    if final:
        factors = [f / denom for f in factors]
    pad = -count % 8
    if pad:
        factors = factors + [jnp.zeros((pad, 128), jnp.float32)]
    columns = jnp.transpose(jnp.concatenate(factors, axis=0))
    numer = None
    for i in range(count):
        term = numer_refs(i) * columns[:rows, i : i + 1]
        numer = term if numer is None else numer + term
    return top, denom, numer


def kernel(
    n, ctx, q_ref, k_hbm, v_hbm, seq_ref, pos_ref, out_ref,
    kbuf, vbuf, qf, bias,
    num1, ml1, rnum1, rml1, num2, ml2, rnum2, rml2, fin,
    ksem, vsem, s1, s1m, r1, r1m, s2, s2m, r2, r2m, s3, r3,
):
    me = lax.axis_index("seq")
    outer_count = n // INNER
    inner = me % INNER
    outer = me // INNER
    y = inner // 2
    c = inner % 2
    owners = [inner, y * 2 + (1 - c), (1 - y) * 2 + c, (1 - y) * 2 + (1 - c)]
    order = [2, 3, 1, 0]
    heads_each = KVH // INNER
    width = heads_each * HD
    rows = q_ref.shape[0] * q_ref.shape[1] * (q_ref.shape[2] // HD // KVH)
    group = q_ref.shape[2] // HD // KVH
    seqs = q_ref.shape[1]
    block = heads_each * rows

    kcopies, vcopies = {}, {}
    for j in order:
        columns = pl.ds(pl.multiple_of(owners[j] * width, width), width)
        kcopies[j] = pltpu.make_async_copy(k_hbm.at[:, columns], kbuf.at[j], ksem.at[j])
        kcopies[j].start()
        vcopies[j] = pltpu.make_async_copy(v_hbm.at[:, columns], vbuf.at[j], vsem.at[j])
        vcopies[j].start()

    barrier = pltpu.get_barrier_semaphore()
    plane_peers = {j: outer * INNER + owners[j] for j in (1, 2, 3)}
    chain_peers = {k: ((outer + k) % outer_count) * INNER + inner for k in range(1, outer_count)}
    peers = list(plane_peers.values()) + list(chain_peers.values())
    for peer in peers:
        pl.semaphore_signal(barrier, inc=1, device_id={"seq": peer}, device_id_type=MESH)

    for t in range(2):
        for head in range(KVH * group):
            g, h = head // group, head % group
            base = g * rows + t * group * seqs + h * seqs
            qf[base : base + seqs, :] = q_ref[t, :, head * HD : (head + 1) * HD].astype(jnp.float32)

    slots = k_hbm.shape[0]
    row_ids = lax.broadcasted_iota(jnp.int32, (rows, 128), 0)
    row_seq = row_ids % seqs
    row_step = row_ids // (group * seqs)
    last = jnp.zeros((rows, 128), jnp.int32)
    for s in range(seqs):
        last = jnp.where(row_seq == s, ctx[s], last)
    last = last - 2 + row_step
    for b in range(slots // 128):
        cut = slice(b * 128, (b + 1) * 128)
        owner = jnp.broadcast_to(seq_ref[:, cut], (rows, 128))
        pos = jnp.broadcast_to(pos_ref[:, cut], (rows, 128))
        allowed = (owner == row_seq) & (pos <= last)
        bias[:, cut] = jnp.where(allowed, 0.0, HIDDEN)

    copies1 = []
    for step, j in enumerate(order):
        owner = owners[j]
        kcopies[j].wait()
        stats = []
        probs = []
        for e in range(heads_each):
            start = pl.multiple_of((owner * heads_each + e) * rows, rows)
            q = qf[pl.ds(start, rows), :].astype(jnp.bfloat16)
            scores = lax.dot_general(
                q, kbuf[j, :, e * HD : (e + 1) * HD], (((1,), (1,)), ((), ())),
                preferred_element_type=jnp.float32,
            ) + bias[...]
            m = jnp.max(scores, axis=-1, keepdims=True)
            w = jnp.exp2((scores - m) * SHIFT)
            l = jnp.sum(w, axis=-1, keepdims=True)
            probs.append(w.astype(jnp.bfloat16))
            stats.append((m, l))
        vcopies[j].wait()
        for e in range(heads_each):
            num1[j, e * rows : (e + 1) * rows, :] = jnp.dot(
                probs[e], vbuf[j, :, e * HD : (e + 1) * HD], preferred_element_type=jnp.float32
            ).astype(jnp.bfloat16)
        lane = lax.broadcasted_iota(jnp.int32, (rows, 128), 1)
        packed = [jnp.where(lane == 0, m, l) for m, l in stats]
        packed = packed + [jnp.zeros((128 - block, 128), jnp.float32)]
        ml1[j] = jnp.transpose(jnp.concatenate(packed, axis=0))[:8, :]
        if j:
            if step == 0:
                pl.semaphore_wait(barrier, len(peers))
            for src, dst, ss, rs in ((ml1, rml1, s1m, r1m), (num1, rnum1, s1, r1)):
                copy = pltpu.make_async_remote_copy(
                    src_ref=src.at[j], dst_ref=dst.at[j], send_sem=ss.at[j], recv_sem=rs.at[j],
                    device_id={"seq": plane_peers[j]}, device_id_type=MESH,
                )
                copy.start()
                copies1.append(copy)

    for copy in copies1:
        copy.wait_recv()
    top, denom, numer = scaled_sum(
        lambda i: rml1[i] if i else ml1[0],
        lambda i: (rnum1[i] if i else num1[0]).astype(jnp.float32),
        INNER, block, False,
    )
    ml2[...] = jnp.concatenate([top, denom, jnp.zeros((6, 128), jnp.float32)], axis=0)
    num2[...] = numer.astype(jnp.bfloat16)

    copies2 = []
    for k in range(1, outer_count):
        for src, dst, ss, rs in ((ml2, rml2, s2m, r2m), (num2, rnum2, s2, r2)):
            copy = pltpu.make_async_remote_copy(
                src_ref=src, dst_ref=dst.at[k], send_sem=ss.at[k], recv_sem=rs.at[k],
                device_id={"seq": chain_peers[k]}, device_id_type=MESH,
            )
            copy.start()
            copies2.append(copy)
    for copy in copies2:
        copy.wait_recv()
    _, _, attended = scaled_sum(
        lambda i: rml2[i] if i else ml2[...],
        lambda i: (rnum2[i] if i else num2[...]).astype(jnp.float32),
        outer_count, block, True,
    )
    fin[0] = attended.astype(jnp.bfloat16)

    copies3 = []
    for j in (2, 3, 1):
        copy = pltpu.make_async_remote_copy(
            src_ref=fin.at[0], dst_ref=fin.at[j], send_sem=s3.at[j], recv_sem=r3.at[j],
            device_id={"seq": plane_peers[j]}, device_id_type=MESH,
        )
        copy.start()
        copies3.append((j, copy))

    def place(j):
        for e in range(heads_each):
            for t in range(2):
                for h in range(group):
                    base = e * rows + t * group * seqs + h * seqs
                    start = pl.multiple_of(((owners[j] * heads_each + e) * group + h) * HD, HD)
                    out_ref[t, :, pl.ds(start, HD)] = fin[j, base : base + seqs, :]

    place(0)
    for j, copy in reversed(copies3):
        copy.wait_recv()
        place(j)
    for copy in copies1 + copies2 + [copy for _, copy in copies3]:
        copy.wait_send()


def per_device(n, queries, cache_k, cache_v, context_len, slot_seq, slot_pos):
    slots = cache_k.shape[0]
    seqs = queries.shape[1]
    heads = queries.shape[2] // HD
    rows = 2 * seqs * heads // KVH
    heads_each = KVH // INNER
    block = heads_each * rows
    outer = n // INNER
    vmem = pl.BlockSpec(memory_space=pltpu.VMEM)
    dma = pltpu.SemaphoreType.DMA
    return pl.pallas_call(
        functools.partial(kernel, n),
        out_shape=jax.ShapeDtypeStruct(queries.shape, jnp.bfloat16),
        in_specs=[
            pl.BlockSpec(memory_space=pltpu.SMEM), vmem,
            pl.BlockSpec(memory_space=pl.ANY), pl.BlockSpec(memory_space=pl.ANY), vmem, vmem,
        ],
        out_specs=vmem,
        scratch_shapes=[
            pltpu.VMEM((INNER, slots, heads_each * HD), jnp.bfloat16),
            pltpu.VMEM((INNER, slots, heads_each * HD), jnp.bfloat16),
            pltpu.VMEM((KVH * rows, HD), jnp.float32),
            pltpu.VMEM((rows, slots), jnp.float32),
            pltpu.VMEM((INNER, block, HD), jnp.bfloat16),
            pltpu.VMEM((INNER, 8, 128), jnp.float32),
            pltpu.VMEM((INNER, block, HD), jnp.bfloat16),
            pltpu.VMEM((INNER, 8, 128), jnp.float32),
            pltpu.VMEM((block, HD), jnp.bfloat16),
            pltpu.VMEM((8, 128), jnp.float32),
            pltpu.VMEM((outer, block, HD), jnp.bfloat16),
            pltpu.VMEM((outer, 8, 128), jnp.float32),
            pltpu.VMEM((INNER, block, HD), jnp.bfloat16),
            dma((INNER,)), dma((INNER,)),
            dma((INNER,)), dma((INNER,)), dma((INNER,)), dma((INNER,)),
            dma((outer,)), dma((outer,)), dma((outer,)), dma((outer,)),
            dma((INNER,)), dma((INNER,)),
        ],
        compiler_params=pltpu.CompilerParams(collective_id=0, has_side_effects=True),
    )(context_len, queries, cache_k, cache_v, slot_seq.reshape(1, slots), slot_pos.reshape(1, slots))


def solution(mesh):
    return jax.shard_map(
        functools.partial(per_device, mesh.shape["seq"]),
        mesh=mesh,
        in_specs=(
            P(None, "parts", None),
            P(("parts", "seq"), None),
            P(("parts", "seq"), None),
            P("parts"),
            P(("parts", "seq")),
            P(("parts", "seq")),
        ),
        out_specs=P(None, "parts", None),
        check_vma=False,
    )
```

time: 91.3 us -> 19.4 us (0.21)
  blocking collectives: 42.8 us -> 0 us
  other arithmetic: 18.6 us -> 0 us
  Pallas kernels: 0 us -> 17.7 us
  between operations: 13.5 us -> 0.01 us
  local copies, waits for them, and re-layouts: 10.4 us -> 1.52 us
  matrix products: 3.79 us -> 0 us
  waiting for transfers between devices: 1.29 us -> 0 us
    all_gather x2 -> x0, blocking collectives: 42.8 us -> none  [merged(): everything = jax.tree.map(lambda part: lax.all_gather(part, axis), array)]
    pallas_call x0 -> x1, Pallas kernels: none -> 17.7 us  [per_device(): pl.pallas_call(functools.partial(kernel, n), out_shape=jax.ShapeDtypeStru...]
    add x31 -> x0, other arithmetic: 16.5 us -> none  [the longest x15 16.2 us: combine(): numer_a * factor_a[..., None] + numer_b * factor_b[..., None]]
    unnamed x8 -> x1, local copies, waits for them, and re-layouts: 8.73 us -> 1.52 us
    dot_general x2 -> x0, matrix products: 3.79 us -> none  [the longest x1 2.11 us: shard_terms(): jnp.einsum('tsghn,ngd->tsghd', weights.astype(jnp.bfloat16), value_rows,...]
    all_gather x1 -> x0, waiting for transfers between devices: 1.27 us -> none  [merged(): everything = jax.tree.map(lambda part: lax.all_gather(part, axis), array)]
    slice x3 -> x0, local copies, waits for them, and re-layouts: 0.92 us -> none  [merged(): first = jax.tree.map(lambda part: part[0], everything)]
  transfers between devices with their start and end apart: 1 -> 0, of which waited for: 1 -> 0; matrix products, arithmetic and copies ran while one was open for 1% -> 0% of each run, Pallas kernels for 0% -> 0%
where the time goes in v1:
time: 19.4 us; the launch traced here: 19.2 us
  Pallas kernels  17.7 us (91%)
  local copies, waits for them, and re-layouts  1.52 us (8%)
    pallas_call x1, Pallas kernels, per_device(): pl.pallas_call(functools.partial(kernel, n), out_shape=jax.ShapeDtypeStru...  17.7 us
    unnamed x1, local copies, waits for them, and re-layouts  1.52 us

profile of v1, /device:TPU:0, one launch (start us, length us, event | category | flops | bytes accessed | tf_op | source)
XLA Modules:
  0.0 19.2 jit_solution(8527312257366969196)
XLA Ops:
  0.0 17.7 %shard_map.64 = bf16[2,2,8192]{2,1,0:T(2,128)(2,1)} custom-call(s32[2]{0:T(128)} %ctx.1, bf16[2,2,8192]{2,1,0:T(2,128)(2,1)} %q_ref.1, bf16[2048,1024]{1,0:T(8,128)(2,1)} %k_hbm.1, bf16[2048,1024]{1,0:T(8,128)(2,1)} %v_hbm.1, s32[1,2048]{1,0:T(1,128)} %bitcast.2, s32[1,2048]{1,0:T(1,128)} %bitcast.3), custom_call_target="tpu_custom_call" | custom-call | tf_op jit(solution)/shard_map/pallas_call | solution.py:199
  17.7 1.5 %copy.8 = bf16[2,2,8192]{2,1,0:T(2,128)(2,1)} copy(bf16[2,2,8192]{2,1,0:T(2,128)(2,1)} %shard_map.64) | data formatting | bytes 131072

commit v2 on v1

v2 whole, which is shorter than its diff:
```python
import functools

import jax
import jax.numpy as jnp
from jax import lax
from jax.experimental import pallas as pl
from jax.experimental.pallas import tpu as pltpu
from jax.sharding import PartitionSpec as P

KVH = 8
HD = 128
INNER = 4
LIMIT = 16 << 20
SHIFT = HD ** (-0.5) * 1.4426950408889634
HIDDEN = -1e30
MESH = pl.DeviceIdType.MESH


def rows_to_columns(rows):
    return jnp.transpose(rows)


def scaled_sum(ml, numer_refs, count, rows, final):
    maxima = [ml(i)[0:1, :] for i in range(count)]
    denoms = [ml(i)[1:2, :] for i in range(count)]
    top = functools.reduce(jnp.maximum, maxima)
    factors = [jnp.exp2((m - top) * SHIFT) for m in maxima]
    denom = sum(f * d for f, d in zip(factors, denoms))
    if final:
        factors = [f / denom for f in factors]
    pad = -count % 8
    if pad:
        factors = factors + [jnp.zeros((pad, 128), jnp.float32)]
    columns = jnp.transpose(jnp.concatenate(factors, axis=0))
    numer = None
    for i in range(count):
        term = numer_refs(i) * columns[:rows, i : i + 1]
        numer = term if numer is None else numer + term
    return top, denom, numer


def kernel(
    n, ctx_hbm, q_hbm, k_hbm, v_hbm, seq_hbm, pos_hbm, fin,
    ctx, q_ref, seq_ref, pos_ref, kbuf, vbuf, qf, bias,
    num1, ml1, rnum1, rml1, num2, ml2, rnum2, rml2, own,
    isem, ksem, vsem, s1, s1m, r1, r1m, s2, s2m, r2, r2m, s3, r3,
):
    me = lax.axis_index("seq")
    outer_count = n // INNER
    inner = me % INNER
    outer = me // INNER
    y = inner // 2
    c = inner % 2
    owners = [inner, y * 2 + (1 - c), (1 - y) * 2 + c, (1 - y) * 2 + (1 - c)]
    heads_each = KVH // INNER
    width = heads_each * HD
    rows = q_ref.shape[0] * q_ref.shape[1] * (q_ref.shape[2] // HD // KVH)
    group = q_ref.shape[2] // HD // KVH
    seqs = q_ref.shape[1]
    block = heads_each * rows

    barrier = pltpu.get_barrier_semaphore()
    plane_peers = {j: outer * INNER + owners[j] for j in (1, 2, 3)}
    chain_peers = {k: ((outer + k) % outer_count) * INNER + inner for k in range(1, outer_count)}
    peers = list(plane_peers.values()) + list(chain_peers.values())
    for peer in peers:
        pl.semaphore_signal(barrier, inc=1, device_id={"seq": peer}, device_id_type=MESH)

    inputs = []
    for i, (src, dst) in enumerate(((q_hbm, q_ref), (seq_hbm, seq_ref), (pos_hbm, pos_ref), (ctx_hbm, ctx))):
        copy = pltpu.make_async_copy(src, dst, isem.at[i])
        copy.start()
        inputs.append(copy)
    kcopies, vcopies = {}, {}
    for which, j in (("k", 2), ("k", 3), ("v", 2), ("k", 1), ("v", 3), ("k", 0), ("v", 1), ("v", 0)):
        columns = pl.ds(pl.multiple_of(owners[j] * width, width), width)
        src, dst, sem, kept = (k_hbm, kbuf, ksem, kcopies) if which == "k" else (v_hbm, vbuf, vsem, vcopies)
        kept[j] = pltpu.make_async_copy(src.at[:, columns], dst.at[j], sem.at[j])
        kept[j].start()

    for copy in inputs:
        copy.wait()

    for t in range(2):
        for head in range(KVH * group):
            g, h = head // group, head % group
            base = g * rows + t * group * seqs + h * seqs
            qf[base : base + seqs, :] = q_ref[t, :, head * HD : (head + 1) * HD].astype(jnp.float32)

    slots = k_hbm.shape[0]
    row_ids = lax.broadcasted_iota(jnp.int32, (rows, 128), 0)
    row_seq = row_ids % seqs
    row_step = row_ids // (group * seqs)
    last = jnp.zeros((rows, 128), jnp.int32)
    for s in range(seqs):
        last = jnp.where(row_seq == s, ctx[s], last)
    last = last - 2 + row_step
    for b in range(slots // 128):
        cut = slice(b * 128, (b + 1) * 128)
        owner = jnp.broadcast_to(seq_ref[:, cut], (rows, 128))
        pos = jnp.broadcast_to(pos_ref[:, cut], (rows, 128))
        allowed = (owner == row_seq) & (pos <= last)
        bias[:, cut] = jnp.where(allowed, 0.0, HIDDEN)

    copies1 = []
    waiting = {}
    lane = lax.broadcasted_iota(jnp.int32, (rows, 128), 1)

    def score(j):
        kcopies[j].wait()
        probs = []
        packed = []
        for e in range(heads_each):
            start = pl.multiple_of((owners[j] * heads_each + e) * rows, rows)
            q = qf[pl.ds(start, rows), :].astype(jnp.bfloat16)
            scores = lax.dot_general(
                q, kbuf[j, :, e * HD : (e + 1) * HD], (((1,), (1,)), ((), ())),
                preferred_element_type=jnp.float32,
            ) + bias[...]
            m = jnp.max(scores, axis=-1, keepdims=True)
            w = jnp.exp2((scores - m) * SHIFT)
            l = jnp.sum(w, axis=-1, keepdims=True)
            probs.append(w.astype(jnp.bfloat16))
            packed.append(jnp.where(lane == 0, m, l))
        packed = packed + [jnp.zeros((128 - block, 128), jnp.float32)]
        ml1[j] = jnp.transpose(jnp.concatenate(packed, axis=0))[:2, :]
        waiting[j] = probs

    def send1(src, dst, ss, rs, j):
        copy = pltpu.make_async_remote_copy(
            src_ref=src.at[j], dst_ref=dst.at[j], send_sem=ss.at[j], recv_sem=rs.at[j],
            device_id={"seq": plane_peers[j]}, device_id_type=MESH,
        )
        copy.start()
        copies1.append(copy)

    def gather(j):
        vcopies[j].wait()
        for e in range(heads_each):
            num1[j, e * rows : (e + 1) * rows, :] = jnp.dot(
                waiting[j][e], vbuf[j, :, e * HD : (e + 1) * HD], preferred_element_type=jnp.float32
            ).astype(jnp.bfloat16)
        if j:
            if j == 2:
                pl.semaphore_wait(barrier, len(peers))
            send1(ml1, rml1, s1m, r1m, j)
            send1(num1, rnum1, s1, r1, j)

    score(2)
    score(3)
    gather(2)
    score(1)
    gather(3)
    score(0)
    gather(1)
    gather(0)

    for copy in copies1:
        copy.wait_recv()
    top, denom, numer = scaled_sum(
        lambda i: rml1[i] if i else ml1[0],
        lambda i: (rnum1[i] if i else num1[0]).astype(jnp.float32),
        INNER, block, False,
    )
    ml2[...] = jnp.concatenate([top, denom], axis=0)
    num2[...] = numer.astype(jnp.bfloat16)

    copies2 = []
    for k in range(1, outer_count):
        for src, dst, ss, rs in ((ml2, rml2, s2m, r2m), (num2, rnum2, s2, r2)):
            copy = pltpu.make_async_remote_copy(
                src_ref=src, dst_ref=dst.at[k], send_sem=ss.at[k], recv_sem=rs.at[k],
                device_id={"seq": chain_peers[k]}, device_id_type=MESH,
            )
            copy.start()
            copies2.append(copy)
    for copy in copies2:
        copy.wait_recv()
    _, _, attended = scaled_sum(
        lambda i: rml2[i] if i else ml2[...],
        lambda i: (rnum2[i] if i else num2[...]).astype(jnp.float32),
        outer_count, block, True,
    )
    own[...] = attended.astype(jnp.bfloat16)

    copies3 = []
    for j in (2, 3, 1):
        copy = pltpu.make_async_remote_copy(
            src_ref=own, dst_ref=fin.at[inner], send_sem=s3.at[j], recv_sem=r3.at[j],
            device_id={"seq": plane_peers[j]}, device_id_type=MESH,
        )
        copy.start()
        copies3.append(copy)
    fin[inner] = own[...]
    for copy in copies3:
        copy.wait_recv()
    for copy in copies1 + copies2 + copies3:
        copy.wait_send()


def place(fin, out_ref):
    steps, seqs, _ = out_ref.shape
    block = fin.shape[1]
    heads = fin.shape[0] * block // (steps * seqs)
    group = heads // KVH
    for head in range(heads):
        g, h = head // group, head % group
        for t in range(steps):
            row = g * group * steps * seqs + t * group * seqs + h * seqs
            i, base = row // block, row % block
            out_ref[t, :, head * HD : (head + 1) * HD] = fin[i, base : base + seqs, :]


def per_device(n, queries, cache_k, cache_v, context_len, slot_seq, slot_pos):
    slots = cache_k.shape[0]
    seqs = queries.shape[1]
    heads = queries.shape[2] // HD
    rows = 2 * seqs * heads // KVH
    heads_each = KVH // INNER
    block = heads_each * rows
    outer = n // INNER
    vmem = pl.BlockSpec(memory_space=pltpu.VMEM)
    dma = pltpu.SemaphoreType.DMA
    anywhere = pl.BlockSpec(memory_space=pltpu.HBM)
    attended = pl.pallas_call(
        functools.partial(kernel, n),
        out_shape=jax.ShapeDtypeStruct((INNER, block, HD), jnp.bfloat16),
        in_specs=[anywhere] * 6,
        out_specs=vmem,
        scratch_shapes=[
            pltpu.SMEM((seqs,), jnp.int32),
            pltpu.VMEM(queries.shape, jnp.bfloat16),
            pltpu.VMEM((1, slots), jnp.int32),
            pltpu.VMEM((1, slots), jnp.int32),
            pltpu.VMEM((INNER, slots, heads_each * HD), jnp.bfloat16),
            pltpu.VMEM((INNER, slots, heads_each * HD), jnp.bfloat16),
            pltpu.VMEM((KVH * rows, HD), jnp.float32),
            pltpu.VMEM((rows, slots), jnp.float32),
            pltpu.VMEM((INNER, block, HD), jnp.bfloat16),
            pltpu.VMEM((INNER, 2, 128), jnp.float32),
            pltpu.VMEM((INNER, block, HD), jnp.bfloat16),
            pltpu.VMEM((INNER, 2, 128), jnp.float32),
            pltpu.VMEM((block, HD), jnp.bfloat16),
            pltpu.VMEM((2, 128), jnp.float32),
            pltpu.VMEM((outer, block, HD), jnp.bfloat16),
            pltpu.VMEM((outer, 2, 128), jnp.float32),
            pltpu.VMEM((block, HD), jnp.bfloat16),
            dma((4,)), dma((INNER,)), dma((INNER,)),
            dma((INNER,)), dma((INNER,)), dma((INNER,)), dma((INNER,)),
            dma((outer,)), dma((outer,)), dma((outer,)), dma((outer,)),
            dma((INNER,)), dma((INNER,)),
        ],
        compiler_params=pltpu.CompilerParams(collective_id=0, has_side_effects=True, vmem_limit_bytes=LIMIT),
    )(*[
        pltpu.with_memory_space_constraint(x, pltpu.HBM)
        for x in (context_len, queries, cache_k, cache_v, slot_seq.reshape(1, slots), slot_pos.reshape(1, slots))
    ])
    return pl.pallas_call(
        place,
        out_shape=jax.ShapeDtypeStruct(queries.shape, jnp.bfloat16),
        in_specs=[vmem],
        out_specs=vmem,
        compiler_params=pltpu.CompilerParams(vmem_limit_bytes=4 << 20),
    )(attended)


def solution(mesh):
    return jax.shard_map(
        functools.partial(per_device, mesh.shape["seq"]),
        mesh=mesh,
        in_specs=(
            P(None, "parts", None),
            P(("parts", "seq"), None),
            P(("parts", "seq"), None),
            P("parts"),
            P(("parts", "seq")),
            P(("parts", "seq")),
        ),
        out_specs=P(None, "parts", None),
        check_vma=False,
    )
```

time: 19.4 us -> 18.4 us (0.948)
  local copies, waits for them, and re-layouts: 1.52 us -> 0 us
  Pallas kernels: 17.7 us -> 18.3 us
    unnamed x1 -> x0, local copies, waits for them, and re-layouts: 1.52 us -> none
    pallas_call x0 -> x1, Pallas kernels: none -> 0.71 us  [per_device(): pl.pallas_call(place, out_shape=jax.ShapeDtypeStruct(queries.shape, jnp.b...]
where the time goes in v2:
time: 18.4 us; the launch traced here: 18.3 us
  Pallas kernels  18.3 us (99%)
    pallas_call x1, Pallas kernels, per_device(): pl.pallas_call(functools.partial(kernel, n), out_shape=jax.ShapeDtypeStru...  17.6 us
    pallas_call x1, Pallas kernels, per_device(): pl.pallas_call(place, out_shape=jax.ShapeDtypeStruct(queries.shape, jnp.b...  0.71 us

profile of v2, /device:TPU:0, one launch (start us, length us, event | category | flops | bytes accessed | tf_op | source)
XLA Modules:
  0.0 18.3 jit_solution(1555858796231576557)
XLA Ops:
  0.0 17.6 %shard_map.64.fin = bf16[4,64,128]{2,1,0:T(8,128)(2,1)S(1)} custom-call(s32[2]{0:T(128)} %ctx_hbm.1, bf16[2,2,8192]{2,1,0:T(2,128)(2,1)} %q_hbm.1, bf16[2048,1024]{1,0:T(8,128)(2,1)} %k_hbm.1, bf16[2048,1024]{1,0:T(8,128)(2,1)} %v_hbm.1, s32[1,2048]{1,0:T(1,128)} %bitcast.2, s32[1,2048]{1,0:T(1,128)} %bitcast.3), custom_call_target="tpu_custom_call" | custom-call | tf_op jit(solution)/shard_map/pallas_call | solution.py:225
  17.6 0.7 %shard_map.65 = bf16[2,2,8192]{2,1,0:T(2,128)(2,1)} custom-call(bf16[4,64,128]{2,1,0:T(8,128)(2,1)S(1)} %shard_map.64.fin), custom_call_target="tpu_custom_call" | custom-call | tf_op jit(solution)/shard_map/pallas_call | solution.py:258
